TPU v7x, 128 devices: a whole 4x4x4 slice. The times are simulated.
128 devices in a mesh: pool: 16 (over x_lo, z, core), cp: 8 (over x_hi, y).
Axes of the slice: x: 4 (x_hi: 2, x_lo: 2; x = x_hi * 2 + x_lo), y: 4, z: 4, core: 2. Of those that a mesh axis runs over, the one named last changes fastest.
Arguments:
- queries: bfloat16 [16, 1024, 4096], P('pool', 'cp'), may hold values from -15 to 15
- span_keys: bfloat16 [16, 1024, 512], P('pool', 'cp'), may hold values from -6 to 6
- span_values: bfloat16 [16, 1024, 512], P('pool', 'cp'), may hold values from -6 to 6
- pool_keys: bfloat16 [384, 128, 512], P('pool'), may hold values from -6 to 6
- pool_values: bfloat16 [384, 128, 512], P('pool'), may hold values from -6 to 6
- page_ids: int32 [16, 32], replicated, may hold values from 0 to 383, as said below
- prefix_pages: int32 [16], replicated, may hold values from 1 to 32, as said below
Outputs:
- attended: float32 [16, 1024, 4096], P('pool', 'cp')
Inputs may be any that keep to these rules, and one draw needn't show every extreme that they name: `page_ids`: page p is held by index p // 24 of pool. Among the first prefix_pages[r] entries of a request, one owner holds at most 2 pages, all different; entries beyond that are unused. `prefix_pages`: some request has all 32 entries in use.
All inputs are finite; a program needn't handle non-finite values.
Results may differ from a plain program's by a relative error of at most 0.002.
Values may be sent and summed in bfloat16 or wider, within the bound.
A program may use at most 128 MiB of HBM per device.

v0:
```python
import jax
import jax.numpy as jnp
from jax import lax
from jax.sharding import PartitionSpec as P

HEAD_DIM = 128
HEADS = 32
KV_HEADS = 4
CAP = 2
PAGES_DEV = 24
NEG_FILL = -1e30


def attend(running, queries_grouped4, key_row_set, value_row_set, visible):
    total_rows = key_row_set.shape[0]
    block_len = 512
    blocks = total_rows // block_len
    score_scale = HEAD_DIM ** (-0.5)
    key_blocks = key_row_set.reshape(blocks, block_len, KV_HEADS, HEAD_DIM)
    value_blocks = value_row_set.reshape(blocks, block_len, KV_HEADS, HEAD_DIM)
    vis_blocks = visible.reshape(visible.shape[0], blocks, block_len).transpose(1, 0, 2)

    def block_step(carried, inputs):
        peak, denom, weighted_values = carried
        key_tile, value_tile, vis_block = inputs
        logit_scores = (
            jnp.einsum(
                "swxl,cwl->swxc", queries_grouped4, key_tile, preferred_element_type=jnp.float32
            )
            * score_scale
        )
        live = vis_block[:, None, None, :]
        logit_scores = jnp.where(live, logit_scores, NEG_FILL)
        new_peak = jnp.maximum(peak, jnp.max(logit_scores, axis=-1))
        softmax_weights = jnp.where(live, jnp.exp(logit_scores - new_peak[..., None]), 0.0).astype(
            jnp.bfloat16
        )
        factor = jnp.exp(peak - new_peak)
        denom = denom * factor + jnp.sum(softmax_weights, axis=-1, dtype=jnp.float32)
        weighted_values = weighted_values * factor[..., None] + jnp.einsum(
            "unqy,ynx->unqx", softmax_weights, value_tile, preferred_element_type=jnp.float32
        )
        return ((new_peak, denom, weighted_values), None)

    return lax.scan(block_step, running, (key_blocks, value_blocks, vis_blocks))[0]


def body(queries, span_keys, span_values, pool_keys, pool_values, page_ids, prefix_pages):
    tok_count = queries.shape[1]
    groups = HEADS // KV_HEADS
    width = KV_HEADS * HEAD_DIM
    queries_grouped4 = queries[0].reshape(tok_count, KV_HEADS, groups, HEAD_DIM)
    pool_count = lax.axis_size("pool")
    pool_index = lax.axis_index("pool")
    ctx_index = lax.axis_index("cp")
    slot_count = page_ids.shape[1]
    owners = page_ids // PAGES_DEV
    slot_iota = jnp.arange(slot_count, dtype=jnp.int32)
    live_slots = slot_iota[None, :] < prefix_pages[:, None]
    earlier = slot_iota[None, :] < slot_iota[:, None]
    same_owner = (owners[:, :, None] == owners[:, None, :]) & live_slots[:, None, :] & earlier[None]
    slot_rank = jnp.sum(same_owner.astype(jnp.int32), axis=2)
    held_here = live_slots & (owners == pool_index)
    cap_iota = jnp.arange(CAP, dtype=jnp.int32)
    picked = held_here[:, None, :] & (slot_rank[:, None, :] == cap_iota[None, :, None])
    local_pages = jnp.sum(jnp.where(picked, page_ids[:, None, :] % PAGES_DEV, 0), axis=2)
    own_owners = lax.dynamic_index_in_dim(owners, pool_index, 0, keepdims=False)
    own_live = lax.dynamic_index_in_dim(live_slots, pool_index, 0, keepdims=False)
    owner_iota = jnp.arange(pool_count, dtype=jnp.int32)
    per_owner = jnp.sum(
        ((own_owners[None, :] == owner_iota[:, None]) & own_live[None, :]).astype(jnp.int32), axis=1
    )
    usable = cap_iota[None, :] < per_owner[:, None]
    empty = (
        jnp.full((tok_count, KV_HEADS, groups), NEG_FILL, jnp.float32),
        jnp.zeros((tok_count, KV_HEADS, groups), jnp.float32),
        jnp.zeros((tok_count, KV_HEADS, groups, HEAD_DIM), jnp.float32),
    )
    query_pos = ctx_index * tok_count + jnp.arange(tok_count, dtype=jnp.int32)
    key_piece = lax.all_gather(span_keys, "cp", axis=1, tiled=True)
    value_piece = lax.all_gather(span_values, "cp", axis=1, tiled=True)
    piece_len = key_piece.shape[1]
    key_pos = jnp.arange(piece_len, dtype=jnp.int32)
    visible = key_pos[None, :] <= query_pos[:, None]
    local_state = attend(empty, queries_grouped4, key_piece[0], value_piece[0], visible)
    fetched_keys, fetched_values = (
        lax.all_to_all(pool_keys[local_pages], "pool", split_axis=0, concat_axis=0, tiled=True),
        lax.all_to_all(pool_values[local_pages], "pool", split_axis=0, concat_axis=0, tiled=True),
    )
    part_len = fetched_keys.shape[2]
    visible = jnp.broadcast_to(usable[:, :, None], (pool_count, CAP, part_len)).reshape(1, -1)
    prefix_state = attend(
        empty,
        queries_grouped4,
        fetched_keys.reshape(-1, width),
        fetched_values.reshape(-1, width),
        visible,
    )
    peak_one, denom_one, mixed_one = local_state
    peak_two, denom_two, mixed_two = prefix_state
    peak = jnp.maximum(peak_one, peak_two)
    factor_one = jnp.exp(peak_one - peak)
    factor_two = jnp.exp(peak_two - peak)
    denom = denom_one * factor_one + denom_two * factor_two
    weighted_values = mixed_one * factor_one[..., None] + mixed_two * factor_two[..., None]
    attended = weighted_values / denom[..., None]
    return attended.reshape(1, tok_count, HEADS * HEAD_DIM)


def solution(mesh):
    in_specs = (
        P("pool", "cp", None),
        P("pool", "cp", None),
        P("pool", "cp", None),
        P("pool", None, None),
        P("pool", None, None),
        P(),
        P(),
    )
    out_specs = P("pool", "cp", None)
    return jax.shard_map(body, mesh=mesh, in_specs=in_specs, out_specs=out_specs, check_vma=False)
```

profile of v0, /device:TPU:103, one launch (start us, length us, event | category | flops | bytes accessed | tf_op | source)
XLA Modules:
  0.0 374.7 jit_solution(9860635105908914886)
XLA Ops:
  11.8 6.0 %all-to-all-start = ((bf16[16,2,128,512]{3,2,1,0:T(8,128)(2,1)}), bf16[16,2,128,512]{3,2,1,0:T(8,128)(2,1)}, u32[]{:S(2)}, u32[]{:S(2)}) async-start(bf16[16,2,128,512]{3,2,1,0:T(8,128)(2,1)} %bitcast.101), calls=%async_computation | async-start | bytes 8388608 | tf_op jit(solution)/shard_map/all_to_all | solution.py:87
  25.0 46.9 %all-gather.5.cloned.1.call-done = bf16[1,1024,512]{2,1,0:T(8,128)(2,1)} async-done(((bf16[1,128,512]{2,1,0:T(8,128)(2,1)}), bf16[1,1024,512]{2,1,0:T(8,128)(2,1)}) %all-gather.5.cloned.1.call-update) | async-done | bytes 1048592 | tf_op jit(solution)/shard_map/all_gather | solution.py:81
  74.0 44.0 %all-gather.3.cloned.1.call-done = bf16[1,1024,512]{2,1,0:T(8,128)(2,1)} async-done(((bf16[1,128,512]{2,1,0:T(8,128)(2,1)}), bf16[1,1024,512]{2,1,0:T(8,128)(2,1)}) %all-gather.3.cloned.1.call-update) | async-done | bytes 1048592 | tf_op jit(solution)/shard_map/all_gather | solution.py:80
  120.2 7.5 %all-to-all-start.1 = ((bf16[16,2,128,512]{3,2,1,0:T(8,128)(2,1)}), bf16[16,2,128,512]{3,2,1,0:T(8,128)(2,1)}, u32[]{:S(2)}, u32[]{:S(2)}) async-start(bf16[16,2,128,512]{3,2,1,0:T(8,128)(2,1)} %bitcast.100), calls=%async_computation.1 | async-start | bytes 8388608 | tf_op jit(solution)/shard_map/all_to_all | solution.py:88
  127.7 36.7 %while.30 = (s32[]{:T(128)}, f32[128,4,8]{0,2,1:T(8,128)S(1)}, f32[128,4,8]{0,2,1:T(8,128)S(1)}, f32[128,4,8,128]{0,3,2,1:T(8,128)}, pred[2,128,512]{1,2,0:T(8,1...) while((s32[]{:T(128)}, f32[128,4,8]{0,2,1:T(8,128)S(1)}, ...), condition=%wide.region_3.4_spmd.clone, body=%wide.region_0.0_spmd.clone.sunk | while | flops 1106792448 | bytes 35192952 | solution.py:45
  138.7 7.0 %bitcast_add_fusion.4 = f32[128,4,8,128]{0,3,2,1:T(8,128)} fusion(f32[128,4,8,128]{0,3,2,1:T(8,128)} %get-tuple-element.406, f32[128,4,8]{0,2,1:T(8,128)S(1)} %get-tuple-element.345, pred[]{:T(512)S(6)} %compare.6, bf16[1,512,4,128]{1,3,2,0:T(8,128)(2,1)S(1)} %copy.60, f32[4,512,128,8]{2,1,3,0:T(8,128)} %get-tuple-element.343, ...), kind=kOutput, calls=%fused_computation.6.clone.1 | convolution fusion | flops 548929536 | bytes 13205505 | tf_op jit(solution)/shard_map/while/body/eval_jaxpr/unqy,ynx->unqx/dot_general | solution.py:40
  156.8 7.6 %bitcast_add_fusion.4 = f32[128,4,8,128]{0,3,2,1:T(8,128)} fusion(f32[128,4,8,128]{0,3,2,1:T(8,128)} %get-tuple-element.406, f32[128,4,8]{0,2,1:T(8,128)S(1)} %get-tuple-element.345, pred[]{:T(512)S(6)} %compare.6, bf16[1,512,4,128]{1,3,2,0:T(8,128)(2,1)S(1)} %copy.60, f32[4,512,128,8]{2,1,3,0:T(8,128)} %get-tuple-element.343, ...), kind=kOutput, calls=%fused_computation.6.clone.1 | convolution fusion | flops 548929536 | bytes 13205505 | tf_op jit(solution)/shard_map/while/body/eval_jaxpr/unqy,ynx->unqx/dot_general | solution.py:40
  164.4 7.0 %reshape_reshape.6 = bf16[8,512,4,128]{3,2,1,0:T(4,128)(2,1)} reshape(bf16[16,2,128,512]{3,2,1,0:T(8,128)(2,1)} %all-to-all-done) | data formatting | bytes 8388608 | tf_op jit(solution)/shard_map/reshape;reshape | solution.py:19
  171.3 18.5 %all-to-all-done.1 = bf16[16,2,128,512]{3,2,1,0:T(8,128)(2,1)} async-done(((bf16[16,2,128,512]{3,2,1,0:T(8,128)(2,1)}), bf16[16,2,128,512]{3,2,1,0:T(8,128)(2,1)}, u32[]{:S(2)}, u32[]{:S(2)}) %all-to-all-start.1) | async-done | bytes 4194336 | tf_op jit(solution)/shard_map/all_to_all | solution.py:88
  189.8 6.9 %reshape_reshape.7 = bf16[8,512,4,128]{3,2,1,0:T(4,128)(2,1)} reshape(bf16[16,2,128,512]{3,2,1,0:T(8,128)(2,1)} %all-to-all-done.1) | data formatting | bytes 8388608 | tf_op jit(solution)/shard_map/reshape;reshape | solution.py:20
  196.7 163.8 %while.31 = (s32[]{:T(128)}, f32[128,4,8]{0,2,1:T(8,128)S(1)}, f32[128,4,8]{0,2,1:T(8,128)S(1)}, f32[128,4,8,128]{0,3,2,1:T(8,128)}, pred[8,1,512]{2,1,0:T(4,128...) while((s32[]{:T(128)}, f32[128,4,8]{0,2,1:T(8,128)S(1)}, ...), condition=%wide.region_10.11_spmd.clone, body=%wide.region_7.10_spmd.clone.sunk | while | flops 1096306688 | bytes 51628208 | solution.py:45
  199.1 4.6 %bitcast_reduce_fusion.2 = (f32[128,4,8]{0,2,1:T(8,128)S(1)}, f32[4,512,128,8]{2,1,3,0:T(8,128)}) fusion(pred[512]{0:T(512)(128)(4,1)S(1)} %dynamic-slice_reduce_fusion.2, bf16[128,4,8,128]{3,0,2,1:T(8,128)(2,1)S(1)} %get-tuple-element.389, bf16[1,512,4,128]{3,2,1,0:T(4,128)(2,1)S(1)} %get-tuple-element.355), kind=kOutput, calls=%fused_computation.19.clone.1 | convolution fusion | flops 543158272 | bytes 9978368 | tf_op jit(solution)/shard_map/while/body/eval_jaxpr/swxl,cwl->swxc/dot_general | solution.py:27
  203.7 6.5 %convert_reduce_fusion.7 = (f32[128,4,8]{0,2,1:T(8,128)S(1)}, bf16[128,4,8,512]{0,3,2,1:T(8,128)(2,1)}) fusion(f32[128,4,8]{0,2,1:T(8,128)S(1)} %select_maximum_fusion.5, f32[4,512,128,8]{2,1,3,0:T(8,128)} %get-tuple-element.357, pred[512]{0:T(512)(128)(4,1)S(1)} %dynamic-slice_reduce_fusion.2), kind=kLoop, calls=%fused_computation.23.clone.1 | loop fusion | flops 14675968 | bytes 12616192 | tf_op jit(solution)/shard_map/while/body/eval_jaxpr/reduce_sum | solution.py:39
  219.6 4.6 %bitcast_reduce_fusion.2 = (f32[128,4,8]{0,2,1:T(8,128)S(1)}, f32[4,512,128,8]{2,1,3,0:T(8,128)}) fusion(pred[512]{0:T(512)(128)(4,1)S(1)} %dynamic-slice_reduce_fusion.2, bf16[128,4,8,128]{3,0,2,1:T(8,128)(2,1)S(1)} %get-tuple-element.389, bf16[1,512,4,128]{3,2,1,0:T(4,128)(2,1)S(1)} %get-tuple-element.355), kind=kOutput, calls=%fused_computation.19.clone.1 | convolution fusion | flops 543158272 | bytes 9978368 | tf_op jit(solution)/shard_map/while/body/eval_jaxpr/swxl,cwl->swxc/dot_general | solution.py:27
  224.2 6.5 %convert_reduce_fusion.7 = (f32[128,4,8]{0,2,1:T(8,128)S(1)}, bf16[128,4,8,512]{0,3,2,1:T(8,128)(2,1)}) fusion(f32[128,4,8]{0,2,1:T(8,128)S(1)} %select_maximum_fusion.5, f32[4,512,128,8]{2,1,3,0:T(8,128)} %get-tuple-element.357, pred[512]{0:T(512)(128)(4,1)S(1)} %dynamic-slice_reduce_fusion.2), kind=kLoop, calls=%fused_computation.23.clone.1 | loop fusion | flops 14675968 | bytes 12616192 | tf_op jit(solution)/shard_map/while/body/eval_jaxpr/reduce_sum | solution.py:39
  240.0 4.6 %bitcast_reduce_fusion.2 = (f32[128,4,8]{0,2,1:T(8,128)S(1)}, f32[4,512,128,8]{2,1,3,0:T(8,128)}) fusion(pred[512]{0:T(512)(128)(4,1)S(1)} %dynamic-slice_reduce_fusion.2, bf16[128,4,8,128]{3,0,2,1:T(8,128)(2,1)S(1)} %get-tuple-element.389, bf16[1,512,4,128]{3,2,1,0:T(4,128)(2,1)S(1)} %get-tuple-element.355), kind=kOutput, calls=%fused_computation.19.clone.1 | convolution fusion | flops 543158272 | bytes 9978368 | tf_op jit(solution)/shard_map/while/body/eval_jaxpr/swxl,cwl->swxc/dot_general | solution.py:27
  244.6 6.5 %convert_reduce_fusion.7 = (f32[128,4,8]{0,2,1:T(8,128)S(1)}, bf16[128,4,8,512]{0,3,2,1:T(8,128)(2,1)}) fusion(f32[128,4,8]{0,2,1:T(8,128)S(1)} %select_maximum_fusion.5, f32[4,512,128,8]{2,1,3,0:T(8,128)} %get-tuple-element.357, pred[512]{0:T(512)(128)(4,1)S(1)} %dynamic-slice_reduce_fusion.2), kind=kLoop, calls=%fused_computation.23.clone.1 | loop fusion | flops 14675968 | bytes 12616192 | tf_op jit(solution)/shard_map/while/body/eval_jaxpr/reduce_sum | solution.py:39
  260.5 4.6 %bitcast_reduce_fusion.2 = (f32[128,4,8]{0,2,1:T(8,128)S(1)}, f32[4,512,128,8]{2,1,3,0:T(8,128)}) fusion(pred[512]{0:T(512)(128)(4,1)S(1)} %dynamic-slice_reduce_fusion.2, bf16[128,4,8,128]{3,0,2,1:T(8,128)(2,1)S(1)} %get-tuple-element.389, bf16[1,512,4,128]{3,2,1,0:T(4,128)(2,1)S(1)} %get-tuple-element.355), kind=kOutput, calls=%fused_computation.19.clone.1 | convolution fusion | flops 543158272 | bytes 9978368 | tf_op jit(solution)/shard_map/while/body/eval_jaxpr/swxl,cwl->swxc/dot_general | solution.py:27
  265.1 6.5 %convert_reduce_fusion.7 = (f32[128,4,8]{0,2,1:T(8,128)S(1)}, bf16[128,4,8,512]{0,3,2,1:T(8,128)(2,1)}) fusion(f32[128,4,8]{0,2,1:T(8,128)S(1)} %select_maximum_fusion.5, f32[4,512,128,8]{2,1,3,0:T(8,128)} %get-tuple-element.357, pred[512]{0:T(512)(128)(4,1)S(1)} %dynamic-slice_reduce_fusion.2), kind=kLoop, calls=%fused_computation.23.clone.1 | loop fusion | flops 14675968 | bytes 12616192 | tf_op jit(solution)/shard_map/while/body/eval_jaxpr/reduce_sum | solution.py:39
  281.0 4.6 %bitcast_reduce_fusion.2 = (f32[128,4,8]{0,2,1:T(8,128)S(1)}, f32[4,512,128,8]{2,1,3,0:T(8,128)}) fusion(pred[512]{0:T(512)(128)(4,1)S(1)} %dynamic-slice_reduce_fusion.2, bf16[128,4,8,128]{3,0,2,1:T(8,128)(2,1)S(1)} %get-tuple-element.389, bf16[1,512,4,128]{3,2,1,0:T(4,128)(2,1)S(1)} %get-tuple-element.355), kind=kOutput, calls=%fused_computation.19.clone.1 | convolution fusion | flops 543158272 | bytes 9978368 | tf_op jit(solution)/shard_map/while/body/eval_jaxpr/swxl,cwl->swxc/dot_general | solution.py:27
  285.6 6.5 %convert_reduce_fusion.7 = (f32[128,4,8]{0,2,1:T(8,128)S(1)}, bf16[128,4,8,512]{0,3,2,1:T(8,128)(2,1)}) fusion(f32[128,4,8]{0,2,1:T(8,128)S(1)} %select_maximum_fusion.5, f32[4,512,128,8]{2,1,3,0:T(8,128)} %get-tuple-element.357, pred[512]{0:T(512)(128)(4,1)S(1)} %dynamic-slice_reduce_fusion.2), kind=kLoop, calls=%fused_computation.23.clone.1 | loop fusion | flops 14675968 | bytes 12616192 | tf_op jit(solution)/shard_map/while/body/eval_jaxpr/reduce_sum | solution.py:39
  306.0 6.5 %convert_reduce_fusion.7 = (f32[128,4,8]{0,2,1:T(8,128)S(1)}, bf16[128,4,8,512]{0,3,2,1:T(8,128)(2,1)}) fusion(f32[128,4,8]{0,2,1:T(8,128)S(1)} %select_maximum_fusion.5, f32[4,512,128,8]{2,1,3,0:T(8,128)} %get-tuple-element.357, pred[512]{0:T(512)(128)(4,1)S(1)} %dynamic-slice_reduce_fusion.2), kind=kLoop, calls=%fused_computation.23.clone.1 | loop fusion | flops 14675968 | bytes 12616192 | tf_op jit(solution)/shard_map/while/body/eval_jaxpr/reduce_sum | solution.py:39
  326.5 6.5 %convert_reduce_fusion.7 = (f32[128,4,8]{0,2,1:T(8,128)S(1)}, bf16[128,4,8,512]{0,3,2,1:T(8,128)(2,1)}) fusion(f32[128,4,8]{0,2,1:T(8,128)S(1)} %select_maximum_fusion.5, f32[4,512,128,8]{2,1,3,0:T(8,128)} %get-tuple-element.357, pred[512]{0:T(512)(128)(4,1)S(1)} %dynamic-slice_reduce_fusion.2), kind=kLoop, calls=%fused_computation.23.clone.1 | loop fusion | flops 14675968 | bytes 12616192 | tf_op jit(solution)/shard_map/while/body/eval_jaxpr/reduce_sum | solution.py:39
  347.0 6.5 %convert_reduce_fusion.7 = (f32[128,4,8]{0,2,1:T(8,128)S(1)}, bf16[128,4,8,512]{0,3,2,1:T(8,128)(2,1)}) fusion(f32[128,4,8]{0,2,1:T(8,128)S(1)} %select_maximum_fusion.5, f32[4,512,128,8]{2,1,3,0:T(8,128)} %get-tuple-element.357, pred[512]{0:T(512)(128)(4,1)S(1)} %dynamic-slice_reduce_fusion.2), kind=kLoop, calls=%fused_computation.23.clone.1 | loop fusion | flops 14675968 | bytes 12616192 | tf_op jit(solution)/shard_map/while/body/eval_jaxpr/reduce_sum | solution.py:39
  (151 shorter events, 134.5 us)
Async XLA Ops:
  6.5 2.5 copy-start
  11.8 7.9 %copy-start.4 = (bf16[24,128,512]{2,1,0:T(8,128)(2,1)S(1)}, bf16[24,128,512]{2,1,0:T(8,128)(2,1)}, u32[]{:S(2)}) copy-start(bf16[24,128,512]{2,1,0:T(8,128)(2,1)} %param.15) | copy-start | bytes 9437188
  11.8 108.3 %all-to-all-start = ((bf16[16,2,128,512]{3,2,1,0:T(8,128)(2,1)}), bf16[16,2,128,512]{3,2,1,0:T(8,128)(2,1)}, u32[]{:S(2)}, u32[]{:S(2)}) async-start(bf16[16,2,128,512]{3,2,1,0:T(8,128)(2,1)} %bitcast.101), calls=%async_computation | async-start | bytes 8388608 | tf_op jit(solution)/shard_map/all_to_all | solution.py:87
  17.8 54.1 %all-gather.5.cloned.1.call-start = ((), (), s32[]{:S(2)}) async-start(), calls=%async_computation.3 | async-start | bytes 1179648 | tf_op jit(solution)/shard_map/all_gather | solution.py:81
  18.5 99.5 %all-gather.3.cloned.1.call-start = ((), (), s32[]{:S(2)}) async-start(), calls=%async_computation.2 | async-start | bytes 1179648 | tf_op jit(solution)/shard_map/all_gather | solution.py:80
  120.2 69.6 %all-to-all-start.1 = ((bf16[16,2,128,512]{3,2,1,0:T(8,128)(2,1)}), bf16[16,2,128,512]{3,2,1,0:T(8,128)(2,1)}, u32[]{:S(2)}, u32[]{:S(2)}) async-start(bf16[16,2,128,512]{3,2,1,0:T(8,128)(2,1)} %bitcast.100), calls=%async_computation.1 | async-start | bytes 8388608 | tf_op jit(solution)/shard_map/all_to_all | solution.py:88
  203.7 8.6 %copy-start.2 = (f32[128,4,8,128]{0,3,2,1:T(8,128)S(1)}, f32[128,4,8,128]{0,3,2,1:T(8,128)}, u32[]{:S(2)}) copy-start(f32[128,4,8,128]{0,3,2,1:T(8,128)} %get-tuple-element.376) | copy-start | bytes 6291460 | tf_op jit(solution)/shard_map/while
  215.9 1.3 copy-start.3
  224.2 8.6 %copy-start.2 = (f32[128,4,8,128]{0,3,2,1:T(8,128)S(1)}, f32[128,4,8,128]{0,3,2,1:T(8,128)}, u32[]{:S(2)}) copy-start(f32[128,4,8,128]{0,3,2,1:T(8,128)} %get-tuple-element.376) | copy-start | bytes 6291460 | tf_op jit(solution)/shard_map/while
  236.3 1.3 copy-start.3
  244.6 8.6 %copy-start.2 = (f32[128,4,8,128]{0,3,2,1:T(8,128)S(1)}, f32[128,4,8,128]{0,3,2,1:T(8,128)}, u32[]{:S(2)}) copy-start(f32[128,4,8,128]{0,3,2,1:T(8,128)} %get-tuple-element.376) | copy-start | bytes 6291460 | tf_op jit(solution)/shard_map/while
  256.8 1.3 copy-start.3
  265.1 8.6 %copy-start.2 = (f32[128,4,8,128]{0,3,2,1:T(8,128)S(1)}, f32[128,4,8,128]{0,3,2,1:T(8,128)}, u32[]{:S(2)}) copy-start(f32[128,4,8,128]{0,3,2,1:T(8,128)} %get-tuple-element.376) | copy-start | bytes 6291460 | tf_op jit(solution)/shard_map/while
  277.3 1.3 copy-start.3
  285.6 8.6 %copy-start.2 = (f32[128,4,8,128]{0,3,2,1:T(8,128)S(1)}, f32[128,4,8,128]{0,3,2,1:T(8,128)}, u32[]{:S(2)}) copy-start(f32[128,4,8,128]{0,3,2,1:T(8,128)} %get-tuple-element.376) | copy-start | bytes 6291460 | tf_op jit(solution)/shard_map/while
  297.8 1.3 copy-start.3
  306.0 8.6 %copy-start.2 = (f32[128,4,8,128]{0,3,2,1:T(8,128)S(1)}, f32[128,4,8,128]{0,3,2,1:T(8,128)}, u32[]{:S(2)}) copy-start(f32[128,4,8,128]{0,3,2,1:T(8,128)} %get-tuple-element.376) | copy-start | bytes 6291460 | tf_op jit(solution)/shard_map/while
  318.2 1.3 copy-start.3
  326.5 8.6 %copy-start.2 = (f32[128,4,8,128]{0,3,2,1:T(8,128)S(1)}, f32[128,4,8,128]{0,3,2,1:T(8,128)}, u32[]{:S(2)}) copy-start(f32[128,4,8,128]{0,3,2,1:T(8,128)} %get-tuple-element.376) | copy-start | bytes 6291460 | tf_op jit(solution)/shard_map/while
  338.7 1.3 copy-start.3
  347.0 8.6 %copy-start.2 = (f32[128,4,8,128]{0,3,2,1:T(8,128)S(1)}, f32[128,4,8,128]{0,3,2,1:T(8,128)}, u32[]{:S(2)}) copy-start(f32[128,4,8,128]{0,3,2,1:T(8,128)} %get-tuple-element.376) | copy-start | bytes 6291460 | tf_op jit(solution)/shard_map/while
  359.2 1.3 copy-start.3
  360.5 7.4 %copy-start.1 = (bf16[24,128,512]{2,1,0:T(8,128)(2,1)S(1)}, bf16[24,128,512]{2,1,0:T(8,128)(2,1)}, u32[]{:S(2)}) copy-start(bf16[24,128,512]{2,1,0:T(8,128)(2,1)} %param.14) | copy-start | bytes 9437188
Sparse Core Ops, SparseCore 0:
  21.0 50.8 all-gather.4
  74.2 43.7 all-gather.2
where the time goes:
time: 376 us; the launch traced here: 375 us
  waiting for transfers between devices  111 us (30%)
  matrix products  88.7 us (24%)
  local copies, waits for them, and re-layouts  79.4 us (21%)
  other arithmetic  68.5 us (18%)
  starting transfers between devices  13.6 us (4%)
  between operations  13.6 us (4%)
    reduce_sum x10, other arithmetic, block_step(): jnp.sum(softmax_weights, axis=-1, dtype=jnp.float32)  61 us
    all_gather x1, waiting for transfers between devices, body(): value_piece = lax.all_gather(span_values, 'cp', axis=1, tiled=True)  46.9 us
    dot_general x10, matrix products, block_step(): jnp.einsum('swxl,cwl->swxc', queries_grouped4, key_tile, preferred_elemen...  45.8 us
    all_gather x1, waiting for transfers between devices, body(): key_piece = lax.all_gather(span_keys, 'cp', axis=1, tiled=True)  44 us
    dot_general x10, matrix products, block_step(): jnp.einsum('unqy,ynx->unqx', softmax_weights, value_tile, preferred_eleme...  42.9 us
    dynamic_slice x28, local copies, waits for them, and re-layouts, attend(): lax.scan(block_step, running, (key_blocks, value_blocks, vis_blocks))[0]  39.7 us
    all_to_all x1, waiting for transfers between devices, body(): lax.all_to_all(pool_values[local_pages], 'pool', split_axis=0, concat_axi...  18.5 us
    while x42, local copies, waits for them, and re-layouts  10.5 us
  transfers between devices with their start and end apart: 4, of which 3 were waited for; matrix products, arithmetic and copies ran while one was open for 14% of the time, Pallas kernels for 0%

commit v1 on v0

--- a/solution.py
+++ b/solution.py
@@ -77,7 +77,9 @@
         jnp.zeros((tok_count, KV_HEADS, groups, HEAD_DIM), jnp.float32),
     )
     query_pos = ctx_index * tok_count + jnp.arange(tok_count, dtype=jnp.int32)
-    key_piece = lax.all_gather(span_keys, "cp", axis=1, tiled=True)
+    key_piece = jnp.concatenate(
+        lax.all_to_all(jnp.stack([span_keys] * lax.axis_size("cp")), "cp", 0, 0), axis=1
+    )
     value_piece = lax.all_gather(span_values, "cp", axis=1, tiled=True)
     piece_len = key_piece.shape[1]
     key_pos = jnp.arange(piece_len, dtype=jnp.int32)

time: 376 us -> 357 us (0.949)
  waiting for transfers between devices: 111 us -> 86.1 us
  starting transfers between devices: 13.6 us -> 18.2 us
    all_gather x1 -> x0, waiting for transfers between devices: 44 us -> none  [body(): key_piece = lax.all_gather(span_keys, 'cp', axis=1, tiled=True)]
    all_to_all x1, waiting for transfers between devices: 0.01 us -> 13.4 us  [body(): lax.all_to_all(pool_keys[local_pages], 'pool', split_axis=0, concat_axis=...]
    all_to_all x0 -> x1, waiting for transfers between devices: none -> 9.74 us  [body(): lax.all_to_all(jnp.stack([span_keys] * lax.axis_size('cp')), 'cp', 0, 0)]
    all_to_all x0 -> x1, starting transfers between devices: none -> 6.87 us  [body(): lax.all_to_all(jnp.stack([span_keys] * lax.axis_size('cp')), 'cp', 0, 0)]
  transfers between devices with their start and end apart: 4 -> 4, of which waited for: 3 -> 4; matrix products, arithmetic and copies ran while one was open for 14% -> 16% of each run, Pallas kernels for 0% -> 0%
where the time goes in v1:
time: 357 us; the launch traced here: 355 us
  matrix products  88.6 us (25%)
  waiting for transfers between devices  86.1 us (24%)
  local copies, waits for them, and re-layouts  81.3 us (23%)
  other arithmetic  67.3 us (19%)
  starting transfers between devices  18.2 us (5%)
  between operations  13.6 us (4%)
    reduce_sum x10, other arithmetic, block_step(): jnp.sum(softmax_weights, axis=-1, dtype=jnp.float32)  60.1 us
    dot_general x10, matrix products, block_step(): jnp.einsum('swxl,cwl->swxc', queries_grouped4, key_tile, preferred_elemen...  45.7 us
    all_gather x1, waiting for transfers between devices, body(): value_piece = lax.all_gather(span_values, 'cp', axis=1, tiled=True)  43.7 us
    dot_general x10, matrix products, block_step(): jnp.einsum('unqy,ynx->unqx', softmax_weights, value_tile, preferred_eleme...  42.9 us
    dynamic_slice x28, local copies, waits for them, and re-layouts, attend(): lax.scan(block_step, running, (key_blocks, value_blocks, vis_blocks))[0]  39.5 us
    all_to_all x1, waiting for transfers between devices, body(): lax.all_to_all(pool_values[local_pages], 'pool', split_axis=0, concat_axi...  18.5 us
    all_to_all x1, waiting for transfers between devices, body(): lax.all_to_all(pool_keys[local_pages], 'pool', split_axis=0, concat_axis=...  13.4 us
    while x42, local copies, waits for them, and re-layouts  10.5 us
  transfers between devices with their start and end apart: 4, of which 4 were waited for; matrix products, arithmetic and copies ran while one was open for 16% of the time, Pallas kernels for 0%

profile of v1, /device:TPU:103, one launch (start us, length us, event | category | flops | bytes accessed | tf_op | source)
XLA Modules:
  0.0 355.4 jit_solution(14492407672730807978)
XLA Ops:
  8.6 6.9 %all-to-all-start = ((bf16[8,1,128,512]{3,2,1,0:T(8,128)(2,1)}), bf16[8,1,128,512]{3,2,1,0:T(8,128)(2,1)}, u32[]{:S(2)}, u32[]{:S(2)}) async-start(bf16[8,1,128,512]{3,2,1,0:T(8,128)(2,1)} %stack.2), calls=%async_computation | async-start | bytes 2097152 | tf_op jit(solution)/shard_map/all_to_all | solution.py:81
  20.6 9.7 %all-to-all-done = bf16[8,1,128,512]{3,2,1,0:T(8,128)(2,1)} async-done(((bf16[8,1,128,512]{3,2,1,0:T(8,128)(2,1)}), bf16[8,1,128,512]{3,2,1,0:T(8,128)(2,1)}, u32[]{:S(2)}, u32[]{:S(2)}) %all-to-all-start) | async-done | bytes 1048608 | tf_op jit(solution)/shard_map/all_to_all | solution.py:81
  30.3 6.1 %all-to-all-start.1 = ((bf16[16,2,128,512]{3,2,1,0:T(8,128)(2,1)}), bf16[16,2,128,512]{3,2,1,0:T(8,128)(2,1)}, u32[]{:S(2)}, u32[]{:S(2)}) async-start(bf16[16,2,128,512]{3,2,1,0:T(8,128)(2,1)} %bitcast.104), calls=%async_computation.1 | async-start | bytes 8388608 | tf_op jit(solution)/shard_map/all_to_all | solution.py:89
  45.0 43.7 %all-gather.2.cloned.1.call-done = bf16[1,1024,512]{2,1,0:T(8,128)(2,1)} async-done(((bf16[1,128,512]{2,1,0:T(8,128)(2,1)}), bf16[1,1024,512]{2,1,0:T(8,128)(2,1)}) %all-gather.2.cloned.1.call-update) | async-done | bytes 1048592 | tf_op jit(solution)/shard_map/all_gather | solution.py:83
  90.9 13.4 %all-to-all-done.1 = bf16[16,2,128,512]{3,2,1,0:T(8,128)(2,1)} async-done(((bf16[16,2,128,512]{3,2,1,0:T(8,128)(2,1)}), bf16[16,2,128,512]{3,2,1,0:T(8,128)(2,1)}, u32[]{:S(2)}, u32[]{:S(2)}) %all-to-all-start.1) | async-done | bytes 4194336 | tf_op jit(solution)/shard_map/all_to_all | solution.py:89
  104.4 5.2 %all-to-all-start.2 = ((bf16[16,2,128,512]{3,2,1,0:T(8,128)(2,1)}), bf16[16,2,128,512]{3,2,1,0:T(8,128)(2,1)}, u32[]{:S(2)}, u32[]{:S(2)}) async-start(bf16[16,2,128,512]{3,2,1,0:T(8,128)(2,1)} %bitcast.103), calls=%async_computation.2 | async-start | bytes 8388608 | tf_op jit(solution)/shard_map/all_to_all | solution.py:90
  109.5 36.7 %while.30 = (s32[]{:T(128)}, f32[128,4,8]{0,2,1:T(8,128)S(1)}, f32[128,4,8]{0,2,1:T(8,128)S(1)}, f32[128,4,8,128]{0,3,2,1:T(8,128)}, pred[2,128,512]{1,2,0:T(8,1...) while((s32[]{:T(128)}, f32[128,4,8]{0,2,1:T(8,128)S(1)}, ...), condition=%wide.region_3.4_spmd.clone, body=%wide.region_0.0_spmd.clone.sunk | while | flops 1106792448 | bytes 35192952 | solution.py:45
  120.6 7.0 %bitcast_add_fusion.4 = f32[128,4,8,128]{0,3,2,1:T(8,128)} fusion(f32[128,4,8,128]{0,3,2,1:T(8,128)} %get-tuple-element.422, f32[128,4,8]{0,2,1:T(8,128)S(1)} %get-tuple-element.361, pred[]{:T(512)S(6)} %compare.6, bf16[1,512,4,128]{1,3,2,0:T(8,128)(2,1)S(1)} %copy.72, f32[4,512,128,8]{2,1,3,0:T(8,128)} %get-tuple-element.359, ...), kind=kOutput, calls=%fused_computation.6.clone.1 | convolution fusion | flops 548929536 | bytes 13205505 | tf_op jit(solution)/shard_map/while/body/eval_jaxpr/unqy,ynx->unqx/dot_general | solution.py:40
  138.6 7.6 %bitcast_add_fusion.4 = f32[128,4,8,128]{0,3,2,1:T(8,128)} fusion(f32[128,4,8,128]{0,3,2,1:T(8,128)} %get-tuple-element.422, f32[128,4,8]{0,2,1:T(8,128)S(1)} %get-tuple-element.361, pred[]{:T(512)S(6)} %compare.6, bf16[1,512,4,128]{1,3,2,0:T(8,128)(2,1)S(1)} %copy.72, f32[4,512,128,8]{2,1,3,0:T(8,128)} %get-tuple-element.359, ...), kind=kOutput, calls=%fused_computation.6.clone.1 | convolution fusion | flops 548929536 | bytes 13205505 | tf_op jit(solution)/shard_map/while/body/eval_jaxpr/unqy,ynx->unqx/dot_general | solution.py:40
  146.2 6.9 %reshape_reshape.6 = bf16[8,512,4,128]{3,2,1,0:T(4,128)(2,1)} reshape(bf16[16,2,128,512]{3,2,1,0:T(8,128)(2,1)} %all-to-all-done.1) | data formatting | bytes 8388608 | tf_op jit(solution)/shard_map/reshape;reshape | solution.py:19
  153.1 18.5 %all-to-all-done.2 = bf16[16,2,128,512]{3,2,1,0:T(8,128)(2,1)} async-done(((bf16[16,2,128,512]{3,2,1,0:T(8,128)(2,1)}), bf16[16,2,128,512]{3,2,1,0:T(8,128)(2,1)}, u32[]{:S(2)}, u32[]{:S(2)}) %all-to-all-start.2) | async-done | bytes 4194336 | tf_op jit(solution)/shard_map/all_to_all | solution.py:90
  171.6 6.9 %reshape_reshape.7 = bf16[8,512,4,128]{3,2,1,0:T(4,128)(2,1)} reshape(bf16[16,2,128,512]{3,2,1,0:T(8,128)(2,1)} %all-to-all-done.2) | data formatting | bytes 8388608 | tf_op jit(solution)/shard_map/reshape;reshape | solution.py:20
  178.6 162.6 %while.31 = (s32[]{:T(128)}, f32[128,4,8]{0,2,1:T(8,128)S(1)}, f32[128,4,8]{0,2,1:T(8,128)S(1)}, f32[128,4,8,128]{0,3,2,1:T(8,128)}, pred[8,1,512]{2,1,0:T(4,128...) while((s32[]{:T(128)}, f32[128,4,8]{0,2,1:T(8,128)S(1)}, ...), condition=%wide.region_10.11_spmd.clone, body=%wide.region_7.10_spmd.clone.sunk | while | flops 1096306688 | bytes 51628208 | solution.py:45
  180.9 4.6 %bitcast_reduce_fusion.2 = (f32[128,4,8]{0,2,1:T(8,128)S(1)}, f32[4,512,128,8]{2,1,3,0:T(8,128)}) fusion(pred[512]{0:T(512)(128)(4,1)S(1)} %dynamic-slice_reduce_fusion.2, bf16[128,4,8,128]{3,0,2,1:T(8,128)(2,1)S(1)} %get-tuple-element.405, bf16[1,512,4,128]{3,2,1,0:T(4,128)(2,1)S(1)} %get-tuple-element.371), kind=kOutput, calls=%fused_computation.19.clone.1 | convolution fusion | flops 543158272 | bytes 9978368 | tf_op jit(solution)/shard_map/while/body/eval_jaxpr/swxl,cwl->swxc/dot_general | solution.py:27
  185.5 6.4 %convert_reduce_fusion.7 = (f32[128,4,8]{0,2,1:T(8,128)S(1)}, bf16[128,4,8,512]{0,3,2,1:T(8,128)(2,1)}) fusion(f32[128,4,8]{0,2,1:T(8,128)S(1)} %select_maximum_fusion.5, f32[4,512,128,8]{2,1,3,0:T(8,128)} %get-tuple-element.373, pred[512]{0:T(512)(128)(4,1)S(1)} %dynamic-slice_reduce_fusion.2), kind=kLoop, calls=%fused_computation.23.clone.1 | loop fusion | flops 14675968 | bytes 12616192 | tf_op jit(solution)/shard_map/while/body/eval_jaxpr/reduce_sum | solution.py:39
  201.2 4.6 %bitcast_reduce_fusion.2 = (f32[128,4,8]{0,2,1:T(8,128)S(1)}, f32[4,512,128,8]{2,1,3,0:T(8,128)}) fusion(pred[512]{0:T(512)(128)(4,1)S(1)} %dynamic-slice_reduce_fusion.2, bf16[128,4,8,128]{3,0,2,1:T(8,128)(2,1)S(1)} %get-tuple-element.405, bf16[1,512,4,128]{3,2,1,0:T(4,128)(2,1)S(1)} %get-tuple-element.371), kind=kOutput, calls=%fused_computation.19.clone.1 | convolution fusion | flops 543158272 | bytes 9978368 | tf_op jit(solution)/shard_map/while/body/eval_jaxpr/swxl,cwl->swxc/dot_general | solution.py:27
  205.8 6.4 %convert_reduce_fusion.7 = (f32[128,4,8]{0,2,1:T(8,128)S(1)}, bf16[128,4,8,512]{0,3,2,1:T(8,128)(2,1)}) fusion(f32[128,4,8]{0,2,1:T(8,128)S(1)} %select_maximum_fusion.5, f32[4,512,128,8]{2,1,3,0:T(8,128)} %get-tuple-element.373, pred[512]{0:T(512)(128)(4,1)S(1)} %dynamic-slice_reduce_fusion.2), kind=kLoop, calls=%fused_computation.23.clone.1 | loop fusion | flops 14675968 | bytes 12616192 | tf_op jit(solution)/shard_map/while/body/eval_jaxpr/reduce_sum | solution.py:39
  221.6 4.6 %bitcast_reduce_fusion.2 = (f32[128,4,8]{0,2,1:T(8,128)S(1)}, f32[4,512,128,8]{2,1,3,0:T(8,128)}) fusion(pred[512]{0:T(512)(128)(4,1)S(1)} %dynamic-slice_reduce_fusion.2, bf16[128,4,8,128]{3,0,2,1:T(8,128)(2,1)S(1)} %get-tuple-element.405, bf16[1,512,4,128]{3,2,1,0:T(4,128)(2,1)S(1)} %get-tuple-element.371), kind=kOutput, calls=%fused_computation.19.clone.1 | convolution fusion | flops 543158272 | bytes 9978368 | tf_op jit(solution)/shard_map/while/body/eval_jaxpr/swxl,cwl->swxc/dot_general | solution.py:27
  226.1 6.4 %convert_reduce_fusion.7 = (f32[128,4,8]{0,2,1:T(8,128)S(1)}, bf16[128,4,8,512]{0,3,2,1:T(8,128)(2,1)}) fusion(f32[128,4,8]{0,2,1:T(8,128)S(1)} %select_maximum_fusion.5, f32[4,512,128,8]{2,1,3,0:T(8,128)} %get-tuple-element.373, pred[512]{0:T(512)(128)(4,1)S(1)} %dynamic-slice_reduce_fusion.2), kind=kLoop, calls=%fused_computation.23.clone.1 | loop fusion | flops 14675968 | bytes 12616192 | tf_op jit(solution)/shard_map/while/body/eval_jaxpr/reduce_sum | solution.py:39
  246.5 6.4 %convert_reduce_fusion.7 = (f32[128,4,8]{0,2,1:T(8,128)S(1)}, bf16[128,4,8,512]{0,3,2,1:T(8,128)(2,1)}) fusion(f32[128,4,8]{0,2,1:T(8,128)S(1)} %select_maximum_fusion.5, f32[4,512,128,8]{2,1,3,0:T(8,128)} %get-tuple-element.373, pred[512]{0:T(512)(128)(4,1)S(1)} %dynamic-slice_reduce_fusion.2), kind=kLoop, calls=%fused_computation.23.clone.1 | loop fusion | flops 14675968 | bytes 12616192 | tf_op jit(solution)/shard_map/while/body/eval_jaxpr/reduce_sum | solution.py:39
  266.8 6.4 %convert_reduce_fusion.7 = (f32[128,4,8]{0,2,1:T(8,128)S(1)}, bf16[128,4,8,512]{0,3,2,1:T(8,128)(2,1)}) fusion(f32[128,4,8]{0,2,1:T(8,128)S(1)} %select_maximum_fusion.5, f32[4,512,128,8]{2,1,3,0:T(8,128)} %get-tuple-element.373, pred[512]{0:T(512)(128)(4,1)S(1)} %dynamic-slice_reduce_fusion.2), kind=kLoop, calls=%fused_computation.23.clone.1 | loop fusion | flops 14675968 | bytes 12616192 | tf_op jit(solution)/shard_map/while/body/eval_jaxpr/reduce_sum | solution.py:39
  287.1 6.4 %convert_reduce_fusion.7 = (f32[128,4,8]{0,2,1:T(8,128)S(1)}, bf16[128,4,8,512]{0,3,2,1:T(8,128)(2,1)}) fusion(f32[128,4,8]{0,2,1:T(8,128)S(1)} %select_maximum_fusion.5, f32[4,512,128,8]{2,1,3,0:T(8,128)} %get-tuple-element.373, pred[512]{0:T(512)(128)(4,1)S(1)} %dynamic-slice_reduce_fusion.2), kind=kLoop, calls=%fused_computation.23.clone.1 | loop fusion | flops 14675968 | bytes 12616192 | tf_op jit(solution)/shard_map/while/body/eval_jaxpr/reduce_sum | solution.py:39
  307.4 6.4 %convert_reduce_fusion.7 = (f32[128,4,8]{0,2,1:T(8,128)S(1)}, bf16[128,4,8,512]{0,3,2,1:T(8,128)(2,1)}) fusion(f32[128,4,8]{0,2,1:T(8,128)S(1)} %select_maximum_fusion.5, f32[4,512,128,8]{2,1,3,0:T(8,128)} %get-tuple-element.373, pred[512]{0:T(512)(128)(4,1)S(1)} %dynamic-slice_reduce_fusion.2), kind=kLoop, calls=%fused_computation.23.clone.1 | loop fusion | flops 14675968 | bytes 12616192 | tf_op jit(solution)/shard_map/while/body/eval_jaxpr/reduce_sum | solution.py:39
  327.7 6.4 %convert_reduce_fusion.7 = (f32[128,4,8]{0,2,1:T(8,128)S(1)}, bf16[128,4,8,512]{0,3,2,1:T(8,128)(2,1)}) fusion(f32[128,4,8]{0,2,1:T(8,128)S(1)} %select_maximum_fusion.5, f32[4,512,128,8]{2,1,3,0:T(8,128)} %get-tuple-element.373, pred[512]{0:T(512)(128)(4,1)S(1)} %dynamic-slice_reduce_fusion.2), kind=kLoop, calls=%fused_computation.23.clone.1 | loop fusion | flops 14675968 | bytes 12616192 | tf_op jit(solution)/shard_map/while/body/eval_jaxpr/reduce_sum | solution.py:39
  (151 shorter events, 144.6 us)
Async XLA Ops:
  6.5 11.3 %copy-start = (bf16[24,128,512]{2,1,0:T(8,128)(2,1)S(1)}, bf16[24,128,512]{2,1,0:T(8,128)(2,1)}, u32[]{:S(2)}) copy-start(bf16[24,128,512]{2,1,0:T(8,128)(2,1)} %param.14) | copy-start | bytes 9437188
  8.6 21.7 %all-to-all-start = ((bf16[8,1,128,512]{3,2,1,0:T(8,128)(2,1)}), bf16[8,1,128,512]{3,2,1,0:T(8,128)(2,1)}, u32[]{:S(2)}, u32[]{:S(2)}) async-start(bf16[8,1,128,512]{3,2,1,0:T(8,128)(2,1)} %stack.2), calls=%async_computation | async-start | bytes 2097152 | tf_op jit(solution)/shard_map/all_to_all | solution.py:81
  30.3 7.2 %copy-start.4 = (bf16[24,128,512]{2,1,0:T(8,128)(2,1)S(1)}, bf16[24,128,512]{2,1,0:T(8,128)(2,1)}, u32[]{:S(2)}) copy-start(bf16[24,128,512]{2,1,0:T(8,128)(2,1)} %param.15) | copy-start | bytes 9437188
  30.3 74.1 %all-to-all-start.1 = ((bf16[16,2,128,512]{3,2,1,0:T(8,128)(2,1)}), bf16[16,2,128,512]{3,2,1,0:T(8,128)(2,1)}, u32[]{:S(2)}, u32[]{:S(2)}) async-start(bf16[16,2,128,512]{3,2,1,0:T(8,128)(2,1)} %bitcast.104), calls=%async_computation.1 | async-start | bytes 8388608 | tf_op jit(solution)/shard_map/all_to_all | solution.py:89
  36.4 52.3 %all-gather.2.cloned.1.call-start = ((), (), s32[]{:S(2)}) async-start(), calls=%async_computation.3 | async-start | bytes 1179648 | tf_op jit(solution)/shard_map/all_gather | solution.py:83
  104.4 67.3 %all-to-all-start.2 = ((bf16[16,2,128,512]{3,2,1,0:T(8,128)(2,1)}), bf16[16,2,128,512]{3,2,1,0:T(8,128)(2,1)}, u32[]{:S(2)}, u32[]{:S(2)}) async-start(bf16[16,2,128,512]{3,2,1,0:T(8,128)(2,1)} %bitcast.103), calls=%async_computation.2 | async-start | bytes 8388608 | tf_op jit(solution)/shard_map/all_to_all | solution.py:90
  185.5 8.5 %copy-start.2 = (f32[128,4,8,128]{0,3,2,1:T(8,128)S(1)}, f32[128,4,8,128]{0,3,2,1:T(8,128)}, u32[]{:S(2)}) copy-start(f32[128,4,8,128]{0,3,2,1:T(8,128)} %get-tuple-element.392) | copy-start | bytes 6291460 | tf_op jit(solution)/shard_map/while
  197.6 1.3 copy-start.3
  205.8 8.5 %copy-start.2 = (f32[128,4,8,128]{0,3,2,1:T(8,128)S(1)}, f32[128,4,8,128]{0,3,2,1:T(8,128)}, u32[]{:S(2)}) copy-start(f32[128,4,8,128]{0,3,2,1:T(8,128)} %get-tuple-element.392) | copy-start | bytes 6291460 | tf_op jit(solution)/shard_map/while
  217.9 1.3 copy-start.3
  226.1 8.5 %copy-start.2 = (f32[128,4,8,128]{0,3,2,1:T(8,128)S(1)}, f32[128,4,8,128]{0,3,2,1:T(8,128)}, u32[]{:S(2)}) copy-start(f32[128,4,8,128]{0,3,2,1:T(8,128)} %get-tuple-element.392) | copy-start | bytes 6291460 | tf_op jit(solution)/shard_map/while
  238.2 1.3 copy-start.3
  246.5 8.5 %copy-start.2 = (f32[128,4,8,128]{0,3,2,1:T(8,128)S(1)}, f32[128,4,8,128]{0,3,2,1:T(8,128)}, u32[]{:S(2)}) copy-start(f32[128,4,8,128]{0,3,2,1:T(8,128)} %get-tuple-element.392) | copy-start | bytes 6291460 | tf_op jit(solution)/shard_map/while
  258.5 1.3 copy-start.3
  266.8 8.5 %copy-start.2 = (f32[128,4,8,128]{0,3,2,1:T(8,128)S(1)}, f32[128,4,8,128]{0,3,2,1:T(8,128)}, u32[]{:S(2)}) copy-start(f32[128,4,8,128]{0,3,2,1:T(8,128)} %get-tuple-element.392) | copy-start | bytes 6291460 | tf_op jit(solution)/shard_map/while
  278.8 1.3 copy-start.3
  287.1 8.5 %copy-start.2 = (f32[128,4,8,128]{0,3,2,1:T(8,128)S(1)}, f32[128,4,8,128]{0,3,2,1:T(8,128)}, u32[]{:S(2)}) copy-start(f32[128,4,8,128]{0,3,2,1:T(8,128)} %get-tuple-element.392) | copy-start | bytes 6291460 | tf_op jit(solution)/shard_map/while
  299.2 1.3 copy-start.3
  307.4 8.5 %copy-start.2 = (f32[128,4,8,128]{0,3,2,1:T(8,128)S(1)}, f32[128,4,8,128]{0,3,2,1:T(8,128)}, u32[]{:S(2)}) copy-start(f32[128,4,8,128]{0,3,2,1:T(8,128)} %get-tuple-element.392) | copy-start | bytes 6291460 | tf_op jit(solution)/shard_map/while
  319.5 1.3 copy-start.3
  327.7 8.5 %copy-start.2 = (f32[128,4,8,128]{0,3,2,1:T(8,128)S(1)}, f32[128,4,8,128]{0,3,2,1:T(8,128)}, u32[]{:S(2)}) copy-start(f32[128,4,8,128]{0,3,2,1:T(8,128)} %get-tuple-element.392) | copy-start | bytes 6291460 | tf_op jit(solution)/shard_map/while
  339.8 1.3 copy-start.3
  341.1 7.4 %copy-start.1 = (bf16[24,128,512]{2,1,0:T(8,128)(2,1)S(1)}, bf16[24,128,512]{2,1,0:T(8,128)(2,1)}, u32[]{:S(2)}) copy-start(bf16[24,128,512]{2,1,0:T(8,128)(2,1)} %param.14) | copy-start | bytes 9437188
Sparse Core Ops, SparseCore 0:
  39.6 49.1 all-gather.1
